TPU v7x, 256 devices: a whole 4x4x8 slice. The times are simulated.
256 devices in a mesh: outer: 16 (over z, core), inner: 16 (over y, x).
Axes of the slice: x: 4, y: 4, z: 8, core: 2. Of those that a mesh axis runs over, the one named last changes fastest.
Arguments:
- queries: bfloat16 [32768, 4096], P(('outer', 'inner')), may hold values from -48 to 48
- keys: bfloat16 [32768, 1024], P(('outer', 'inner')), may hold values from -20 to 20
- values: bfloat16 [32768, 1024], P(('outer', 'inner')), may hold values from -6 to 6
- ancestors: int32 [256, 8], replicated, may hold values from -1 to 255, as said below
- token_block: int32 [32768], replicated, may hold values from 0 to 255, as said below
- positions: int32 [32768], replicated, may hold values from 0 to 1023, as said below
Outputs:
- attended: bfloat16 [32768, 4096], P(('outer', 'inner'))
Inputs may be any that keep to these rules, and one draw needn't show every extreme that they name: `ancestors`: row b lists the blocks on the path from the root block 0 to block b, root first and b last, then -1; a parent has a smaller number than its child; some row lists 8 blocks. `token_block`: each aligned span of 128 tokens belongs to one block, and every block fills exactly one span; apart from block 0, no two blocks of one root path lie in the same aligned group of 2048 tokens. `positions`: a token's position is 128 times (the number of blocks on its block's root path minus 1) plus its offset within its span.
All inputs are finite; a program needn't handle non-finite values.
Results may differ from a plain program's by a relative error of at most 0.0065.
Values may be sent and summed in bfloat16 or wider, within the bound.
No kernel may reach another device: no remote copies, remote signals or barrier semaphores. Data moves between devices by JAX's collectives and lax.ppermute only.
A program may use at most 128 MiB of HBM per device.

v0:
```python
import jax
import jax.numpy as jnp
from jax import lax
from jax.sharding import PartitionSpec as P

HEADS = 32
KV_HEADS = 8
HEAD_DIM = 128
BLOCK = 128
ANC_MAX = 8
ROTARY_BASE = 500000.0


def rotate(matrix, places, head_count):
    row_count = matrix.shape[0]
    head_width = matrix.shape[1] // head_count
    half_width = head_width // 2
    inverse = ROTARY_BASE ** (-2.0 * jnp.arange(half_width, dtype=jnp.float32) / head_width)
    angles = places.astype(jnp.float32)[:, None] * inverse[None, :]
    cosine = jnp.cos(angles)[:, None, :]
    sine_part = jnp.sin(angles)[:, None, :]
    unfolded = matrix.astype(jnp.float32).reshape(row_count, head_count, head_width)
    leading = unfolded[:, :, :half_width]
    trailing = unfolded[:, :, half_width:]
    turned = jnp.concatenate(
        [leading * cosine - trailing * sine_part, trailing * cosine + leading * sine_part], axis=2
    )
    return turned.reshape(row_count, head_count * head_width).astype(jnp.bfloat16)


def shards(queries, keys, values, ancestors, token_block, positions):
    tok_rows = queries.shape[0]
    span_count = tok_rows // BLOCK
    group_size = HEADS // KV_HEADS
    kv_width = keys.shape[1]
    outer_count = lax.axis_size("outer")
    inner_count = lax.axis_size("inner")
    outer_me = lax.axis_index("outer")
    inner_me = lax.axis_index("inner")
    device_me = outer_me * inner_count + inner_me
    start_row = device_me * tok_rows
    own_places = lax.dynamic_slice_in_dim(positions, start_row, tok_rows)
    rot_q = rotate(queries, own_places, HEADS)
    rot_k = rotate(keys, own_places, KV_HEADS)
    block_count = ancestors.shape[0]
    block_ids = jnp.arange(block_count, dtype=jnp.int32)
    span_blocks = token_block[::BLOCK]
    span_of = jnp.sum(
        jnp.where(span_blocks[:, None] == block_ids[None, :], block_ids[:, None], 0), axis=0
    )
    group_spans = inner_count * span_count
    capacity = 2
    span_ids = jnp.arange(span_count, dtype=jnp.int32)
    slot_ids = jnp.arange(capacity, dtype=jnp.int32)
    bundled = (
        lax.all_gather(rot_k, "inner", axis=0, tiled=True),
        lax.all_gather(values, "inner", axis=0, tiled=True),
    )
    key_blocks = bundled[0].reshape(group_spans, BLOCK, kv_width)
    value_blocks = bundled[1].reshape(group_spans, BLOCK, kv_width)
    dest_outer = jnp.arange(outer_count, dtype=jnp.int32)
    dest_spans = (dest_outer[:, None] * inner_count + inner_me) * span_count + span_ids[None, :]
    dest_lineage = ancestors[span_blocks[dest_spans]]
    lineage_spans = span_of[jnp.maximum(dest_lineage, 0)]
    counted = dest_lineage >= 0
    matches = counted & (lineage_spans // group_spans == outer_me)
    slot_rank = jnp.cumsum(matches.astype(jnp.int32), axis=2) - 1
    local_spans = lineage_spans - outer_me * group_spans
    picked = jnp.sum(
        jnp.where(
            matches[..., None] & (slot_rank[..., None] == slot_ids), local_spans[..., None], 0
        ),
        axis=2,
    )
    send_keys = key_blocks[picked]
    send_values = value_blocks[picked]
    received = (
        lax.all_to_all(send_keys, "outer", split_axis=0, concat_axis=0, tiled=True),
        lax.all_to_all(send_values, "outer", split_axis=0, concat_axis=0, tiled=True),
    )
    own_spans = device_me * span_count + span_ids
    own_lineage = ancestors[span_blocks[own_spans]]
    own_valid = own_lineage >= 0
    own_span_of = span_of[jnp.maximum(own_lineage, 0)]
    own_groups = own_span_of // group_spans
    path_ids = jnp.arange(ANC_MAX, dtype=jnp.int32)
    earlier = path_ids[None, :] < path_ids[:, None]
    same_group = (
        own_valid[:, None, :]
        & (own_groups[:, :, None] == own_groups[:, None, :])
        & earlier[None, :, :]
    )
    own_rank = jnp.minimum(jnp.sum(same_group.astype(jnp.int32), axis=2), capacity - 1)
    slot_index = (own_groups * span_count + span_ids[:, None]) * capacity + own_rank
    slot_total = outer_count * span_count * capacity
    got_keys = received[0].reshape(slot_total, BLOCK, kv_width)[slot_index]
    got_values = received[1].reshape(slot_total, BLOCK, kv_width)[slot_index]
    offsets = jnp.arange(BLOCK, dtype=jnp.int32)
    key_index = (own_span_of[:, :, None] * BLOCK + offsets[None, None, :]).reshape(
        span_count, ANC_MAX * BLOCK
    )
    key_places = positions[key_index]
    query_places = own_places.reshape(span_count, BLOCK)
    allowed = jnp.repeat(own_valid, BLOCK, axis=1)[:, None, :] & (
        key_places[:, None, :] <= query_places[:, :, None]
    )
    query_rows = rot_q.reshape(span_count, BLOCK, KV_HEADS, group_size, HEAD_DIM)
    key_rows = got_keys.reshape(span_count, ANC_MAX * BLOCK, KV_HEADS, HEAD_DIM)
    value_rows = got_values.reshape(span_count, ANC_MAX * BLOCK, KV_HEADS, HEAD_DIM)
    scaling = HEAD_DIM ** (-0.5)
    scores = (
        jnp.einsum("rtkgd,rukd->rtkgu", query_rows, key_rows, preferred_element_type=jnp.float32)
        * scaling
    )
    wide_mask = allowed[:, :, None, None, :]
    top_score = jnp.max(jnp.where(wide_mask, scores, -jnp.inf), axis=4)
    weights = jnp.where(wide_mask, jnp.exp(scores - top_score[..., None]), 0.0)
    totals = jnp.sum(weights, axis=4)
    mixed_sum = jnp.einsum(
        "rtkgu,rukd->rtkgd",
        weights.astype(jnp.bfloat16),
        value_rows,
        preferred_element_type=jnp.float32,
    )
    attended = (
        (mixed_sum / totals[..., None]).reshape(tok_rows, HEADS * HEAD_DIM).astype(jnp.bfloat16)
    )
    return attended


def solution(mesh):
    placed = (
        P(("outer", "inner"), None),
        P(("outer", "inner"), None),
        P(("outer", "inner"), None),
        P(),
        P(),
        P(),
    )
    return jax.shard_map(
        shards, mesh=mesh, in_specs=placed, out_specs=P(("outer", "inner"), None), check_vma=False
    )
```

profile of v0, /device:TPU:1, one launch (start us, length us, event | category | flops | bytes accessed | tf_op | source)
XLA Modules:
  0.0 498.6 jit_solution(17158688067835165841)
XLA Ops:
  6.6 1.0 convert_bitcast_fusion.1
  7.7 0.8 fusion.28
  9.2 0.8 copy.67
  10.0 1.1 slice.15
  12.7 1.3 gather_fusion.2
  14.7 55.4 %all-gather.5.cloned.1.call-done = bf16[2048,1024]{1,0:T(8,128)(2,1)} async-done(((bf16[128,1024]{1,0:T(8,128)(2,1)}), bf16[2048,1024]{1,0:T(8,128)(2,1)}) %all-gather.5.cloned.1.call-update) | async-done | bytes 4194320 | tf_op jit(solution)/shard_map/all_gather | solution.py:56
  70.2 7.0 %gather_fusion.7 = bf16[32,128,1024]{2,1,0:T(8,128)(2,1)} fusion(bf16[16,128,1024]{2,1,0:T(8,128)(2,1)} %bitcast.102, s32[1024]{0:T(1024)S(1)} %pad_clamp_fusion.2), kind=kCustom, calls=%fused_computation.7 | custom fusion | bytes 16777344 | tf_op jit(solution)/shard_map/gather | solution.py:75
  77.1 7.8 %all-to-all-start.1 = ((bf16[16,1,2,128,1024]{4,3,2,1,0:T(8,128)(2,1)}), bf16[16,1,2,128,1024]{4,3,2,1,0:T(8,128)(2,1)}, u32[]{:S(2)}, u32[]{:S(2)}) async-start(bf16[16,1,2,128,1024]{4,3,2,1,0:T(8,128)(2,1)} %bitcast.100), calls=%async_computation.1 | async-start | bytes 16777216 | tf_op jit(solution)/shard_map/all_to_all | solution.py:78
  85.7 58.0 %all-gather.3.cloned.1.call-done = bf16[2048,1024]{1,0:T(8,128)(2,1)} async-done(((bf16[128,1024]{1,0:T(8,128)(2,1)}), bf16[2048,1024]{1,0:T(8,128)(2,1)}) %all-gather.3.cloned.1.call-update) | async-done | bytes 4194320 | tf_op jit(solution)/shard_map/all_gather | solution.py:57
  143.7 6.9 %gather_fusion.3 = bf16[32,128,1024]{2,1,0:T(8,128)(2,1)} fusion(bf16[16,128,1024]{2,1,0:T(8,128)(2,1)} %bitcast.103, s32[1024]{0:T(1024)S(1)} %pad_clamp_fusion.2), kind=kCustom, calls=%fused_computation.3 | custom fusion | bytes 16777344 | tf_op jit(solution)/shard_map/gather | solution.py:76
  150.6 117.7 %all-to-all-done.1 = bf16[16,1,2,128,1024]{4,3,2,1,0:T(8,128)(2,1)} async-done(((bf16[16,1,2,128,1024]{4,3,2,1,0:T(8,128)(2,1)}), bf16[16,1,2,128,1024]{4,3,2,1,0:T(8,128)(2,1)}, u32[]{:S(2)}, u32[]{:S(2)}) %all-to-all-start.1) | async-done | bytes 8388640 | tf_op jit(solution)/shard_map/all_to_all | solution.py:78
  268.3 5.7 %all-to-all-start = ((bf16[16,1,2,128,1024]{4,3,2,1,0:T(8,128)(2,1)}), bf16[16,1,2,128,1024]{4,3,2,1,0:T(8,128)(2,1)}, u32[]{:S(2)}, u32[]{:S(2)}) async-start(bf16[16,1,2,128,1024]{4,3,2,1,0:T(8,128)(2,1)} %bitcast.99), calls=%async_computation | async-start | bytes 16777216 | tf_op jit(solution)/shard_map/all_to_all | solution.py:79
  277.5 6.2 %gather_fusion.6 = s32[1024]{0:T(1024)S(1)} fusion(s32[32768]{0:T(1024)S(1)} %copy-done, s32[1024]{0:T(1024)S(1)} %broadcast_clamp_fusion), kind=kCustom, calls=%fused_computation.6 | custom fusion | bytes 12288 | tf_op jit(solution)/shard_map/gather | solution.py:102
  284.7 0.7 fusion.29
  285.4 2.5 subtract_convert_fusion
  288.9 5.5 %gather_fusion.8 = bf16[8,128,1024]{2,1,0:T(8,128)(2,1)} fusion(bf16[32,128,1024]{2,1,0:T(8,128)(2,1)} %bitcast.20, s32[1024]{0:T(1024)S(1)} %pad_clamp_fusion), kind=kCustom, calls=%fused_computation.8 | custom fusion | bytes 4194336 | tf_op jit(solution)/shard_map/gather | solution.py:96
  294.4 2.2 copy.52
  296.6 160.9 %all-to-all-done = bf16[16,1,2,128,1024]{4,3,2,1,0:T(8,128)(2,1)} async-done(((bf16[16,1,2,128,1024]{4,3,2,1,0:T(8,128)(2,1)}), bf16[16,1,2,128,1024]{4,3,2,1,0:T(8,128)(2,1)}, u32[]{:S(2)}, u32[]{:S(2)}) %all-to-all-start) | async-done | bytes 8388640 | tf_op jit(solution)/shard_map/all_to_all | solution.py:79
  457.5 5.4 %gather_fusion.5 = bf16[8,128,1024]{2,1,0:T(8,128)(2,1)} fusion(bf16[32,128,1024]{2,1,0:T(8,128)(2,1)} %bitcast.6, s32[1024]{0:T(1024)S(1)} %pad_clamp_fusion), kind=kCustom, calls=%fused_computation.5 | custom fusion | bytes 4194336 | tf_op jit(solution)/shard_map/gather | solution.py:97
  462.9 3.6 copy.49
  466.5 7.0 %fusion = (f32[128,8,4]{0,2,1:T(4,128)S(1)}, f32[8,1024,128,4]{2,1,3,0:T(8,128)}) fusion(pred[128,1024]{0,1:T(8,128)(4,1)S(1)} %compare_and_fusion, bf16[128,8,4,128]{3,0,2,1:T(8,128)(2,1)S(1)} %bitcast.107, bf16[1024,8,128,1]{2,1,0,3:T(8,128)(2,1)S(1)} %bitcast.104), kind=kOutput, calls=%fused_computation.11 | convolution fusion | flops 1086320640 | bytes 20070400 | tf_op jit(solution)/shard_map/rtkgd,rukd->rtkgu/dot_general | solution.py:112
  473.5 9.3 %fusion.3 = f32[128,8,4]{0,2,1:T(4,128)S(1)} fusion(f32[8,1024,128,4]{2,1,3,0:T(8,128)} %get-tuple-element.42, f32[128,8,4]{0,2,1:T(4,128)S(1)} %get-tuple-element.41, pred[128,1024]{0,1:T(8,128)(4,1)S(1)} %compare_and_fusion), kind=kLoop, calls=%fused_computation.14 | loop fusion | flops 16773120 | bytes 16941056 | tf_op jit(solution)/shard_map/reduce_sum | solution.py:118
  482.8 7.7 %fusion.9 = bf16[1,128,8,4,128]{1,4,3,2,0:T(8,128)(2,1)S(1)} fusion(f32[128,8,4]{0,2,1:T(4,128)S(1)} %fusion.3, f32[8,1024,128,4]{2,1,3,0:T(8,128)} %get-tuple-element.42, f32[128,8,4]{0,2,1:T(4,128)S(1)} %get-tuple-element.41, pred[128,1024]{0,1:T(8,128)(4,1)S(1)} %compare_and_fusion, bf16[1024,8,128,1]{2,1,0,3:T(8,128)(2,1)S(1)} %bitcast.109), kind=kOutput, calls=%fused_computation.20 | convolution fusion | flops 1091567616 | bytes 20086784 | tf_op jit(solution)/shard_map/rtkgu,rukd->rtkgd/dot_general | solution.py:119
  490.4 1.3 copy.39
  (58 shorter events, 7.4 us)
Async XLA Ops:
  6.5 4.6 copy-start.3
  6.5 63.6 %all-gather.5.cloned.1.call-start = ((), (), s32[]{:S(2)}) async-start(), calls=%async_computation.3 | async-start | bytes 4456448 | tf_op jit(solution)/shard_map/all_gather | solution.py:56
  77.1 191.2 %all-to-all-start.1 = ((bf16[16,1,2,128,1024]{4,3,2,1,0:T(8,128)(2,1)}), bf16[16,1,2,128,1024]{4,3,2,1,0:T(8,128)(2,1)}, u32[]{:S(2)}, u32[]{:S(2)}) async-start(bf16[16,1,2,128,1024]{4,3,2,1,0:T(8,128)(2,1)} %bitcast.100), calls=%async_computation.1 | async-start | bytes 16777216 | tf_op jit(solution)/shard_map/all_to_all | solution.py:78
  84.9 58.7 %all-gather.3.cloned.1.call-start = ((), (), s32[]{:S(2)}) async-start(), calls=%async_computation.2 | async-start | bytes 4456448 | tf_op jit(solution)/shard_map/all_gather | solution.py:57
  268.3 9.2 %copy-start = (s32[32768]{0:T(1024)S(1)}, s32[32768]{0:T(1024)}, u32[]{:S(2)}) copy-start(s32[32768]{0:T(1024)} %param.11) | copy-start | bytes 393220
  268.3 189.1 %all-to-all-start = ((bf16[16,1,2,128,1024]{4,3,2,1,0:T(8,128)(2,1)}), bf16[16,1,2,128,1024]{4,3,2,1,0:T(8,128)(2,1)}, u32[]{:S(2)}, u32[]{:S(2)}) async-start(bf16[16,1,2,128,1024]{4,3,2,1,0:T(8,128)(2,1)} %bitcast.99), calls=%async_computation | async-start | bytes 16777216 | tf_op jit(solution)/shard_map/all_to_all | solution.py:79
  274.1 9.6 %copy-start.2 = (bf16[128,4096]{1,0:T(8,128)(2,1)S(1)}, bf16[128,4096]{1,0:T(8,128)(2,1)}, u32[]{:S(2)}) copy-start(bf16[128,4096]{1,0:T(8,128)(2,1)} %param.6) | copy-start | bytes 3145732
  473.5 9.3 %copy-start.1 = (bf16[128,8,8,128]{3,2,1,0:T(8,128)(2,1)S(1)}, bf16[128,8,8,128]{3,2,1,0:T(8,128)(2,1)}, u32[]{:S(2)}) copy-start(bf16[128,8,8,128]{3,2,1,0:T(8,128)(2,1)} %copy.49) | copy-start | bytes 6291460
Sparse Core Ops, SparseCore 0:
  10.1 60.0 all-gather.4
  88.2 55.4 all-gather.2
where the time goes:
time: 499 us
  waiting for transfers between devices  393 us (79%)
  local copies, waits for them, and re-layouts  45.6 us (9%)
  other arithmetic  16.5 us (3%)
  between operations  15.5 us (3%)
  matrix products  14.7 us (3%)
  starting transfers between devices  13.6 us (3%)
    all_to_all x1, waiting for transfers between devices, shards(): lax.all_to_all(send_values, 'outer', split_axis=0, concat_axis=0, tiled=T...  161 us
    all_to_all x1, waiting for transfers between devices, shards(): lax.all_to_all(send_keys, 'outer', split_axis=0, concat_axis=0, tiled=True)  118 us
    all_gather x1, waiting for transfers between devices, shards(): lax.all_gather(values, 'inner', axis=0, tiled=True)  58 us
    all_gather x1, waiting for transfers between devices, shards(): lax.all_gather(rot_k, 'inner', axis=0, tiled=True)  55.4 us
  transfers between devices with their start and end apart: 4, of which 4 were waited for; matrix products, arithmetic and copies ran while one was open for 6% of the time, Pallas kernels for 0%

commit v1 on v0

--- a/solution.py
+++ b/solution.py
@@ -9,6 +9,29 @@
 BLOCK = 128
 ANC_MAX = 8
 ROTARY_BASE = 500000.0
+
+
+def _pack_lane(content, which_dim):
+    o_now = list(content.shape[1:])
+    o_now[which_dim] *= content.shape[0]
+    return jnp.moveaxis(content, 0, which_dim).reshape(o_now)
+
+
+def play_quotas(local_array, mesh_ax, along_dim):
+    count_all = lax.axis_size(mesh_ax)
+    pool = [(dev_j, (dev_j + 1) % count_all) for dev_j in range(count_all)]
+    met_up, t1 = ([], [])
+    made = [(pp, dd) for dd, pp in pool]
+    for jj in range(count_all - 1):
+        if jj % 2 == 0:
+            met_up.append(lax.ppermute(met_up[-1] if met_up else local_array, mesh_ax, pool))
+        else:
+            t1.append(lax.ppermute(t1[-1] if t1 else local_array, mesh_ax, made))
+    block_now = jnp.stack([*met_up[::-1], local_array, *t1], axis=0)
+    current_arr = lax.axis_index(mesh_ax)
+    lower = current_arr - len(met_up)
+    block_now = block_now[(jnp.arange(count_all) - lower) % count_all]
+    return _pack_lane(block_now, along_dim)
 
 
 def rotate(matrix, places, head_count):
@@ -52,10 +75,7 @@
     capacity = 2
     span_ids = jnp.arange(span_count, dtype=jnp.int32)
     slot_ids = jnp.arange(capacity, dtype=jnp.int32)
-    bundled = (
-        lax.all_gather(rot_k, "inner", axis=0, tiled=True),
-        lax.all_gather(values, "inner", axis=0, tiled=True),
-    )
+    bundled = (lax.all_gather(rot_k, "inner", axis=0, tiled=True), play_quotas(values, "inner", 0))
     key_blocks = bundled[0].reshape(group_spans, BLOCK, kv_width)
     value_blocks = bundled[1].reshape(group_spans, BLOCK, kv_width)
     dest_outer = jnp.arange(outer_count, dtype=jnp.int32)

time: 499 us -> 534 us (1.070)
  starting transfers between devices: 13.6 us -> 58.7 us
  waiting for transfers between devices: 393 us -> 370 us
  local copies, waits for them, and re-layouts: 45.6 us -> 59 us
    all_gather x1 -> x0, waiting for transfers between devices: 58 us -> none  [shards(): lax.all_gather(values, 'inner', axis=0, tiled=True)]
    all_to_all x1, waiting for transfers between devices: 118 us -> 165 us  [shards(): lax.all_to_all(send_keys, 'outer', split_axis=0, concat_axis=0, tiled=True)]
    all_to_all x1, waiting for transfers between devices: 161 us -> 121 us  [shards(): lax.all_to_all(send_values, 'outer', split_axis=0, concat_axis=0, tiled=T...]
    ppermute x0 -> x15, starting transfers between devices: none -> 37.3 us  [the longest x7 35.2 us: play_quotas(): t1.append(lax.ppermute(t1[-1] if t1 else local_array, mesh_ax, made))]
    ppermute x0 -> x15, waiting for transfers between devices: none -> 30.3 us  [the longest x8 26 us: play_quotas(): lax.ppermute(met_up[-1] if met_up else local_array, mesh_ax, pool)]
    unnamed x14 -> x33, local copies, waits for them, and re-layouts: 7.13 us -> 17.5 us
    all_to_all x1, starting transfers between devices: 5.73 us -> 15.7 us  [shards(): lax.all_to_all(send_values, 'outer', split_axis=0, concat_axis=0, tiled=T...]
  transfers between devices with their start and end apart: 4 -> 18, of which waited for: 4 -> 13; matrix products, arithmetic and copies ran while one was open for 6% -> 9% of each run, Pallas kernels for 0% -> 0%
where the time goes in v1:
time: 534 us
  waiting for transfers between devices  370 us (69%)
  local copies, waits for them, and re-layouts  59 us (11%)
  starting transfers between devices  58.7 us (11%)
  other arithmetic  15.6 us (3%)
  between operations  15.6 us (3%)
  matrix products  14.8 us (3%)
    all_to_all x1, waiting for transfers between devices, shards(): lax.all_to_all(send_keys, 'outer', split_axis=0, concat_axis=0, tiled=True)  165 us
    all_to_all x1, waiting for transfers between devices, shards(): lax.all_to_all(send_values, 'outer', split_axis=0, concat_axis=0, tiled=T...  121 us
    all_gather x1, waiting for transfers between devices, shards(): lax.all_gather(rot_k, 'inner', axis=0, tiled=True)  53.5 us
    ppermute x7, starting transfers between devices, play_quotas(): t1.append(lax.ppermute(t1[-1] if t1 else local_array, mesh_ax, made))  35.2 us
    ppermute x8, waiting for transfers between devices, play_quotas(): lax.ppermute(met_up[-1] if met_up else local_array, mesh_ax, pool)  26 us
    unnamed x33, local copies, waits for them, and re-layouts  17.5 us
    all_to_all x1, starting transfers between devices, shards(): lax.all_to_all(send_values, 'outer', split_axis=0, concat_axis=0, tiled=T...  15.7 us
  transfers between devices with their start and end apart: 18, of which 13 were waited for; matrix products, arithmetic and copies ran while one was open for 9% of the time, Pallas kernels for 0%

profile of v1, /device:TPU:1, one launch (start us, length us, event | category | flops | bytes accessed | tf_op | source)
XLA Modules:
  0.0 533.5 jit_solution(17651226226439021557)
XLA Ops:
  8.6 8.1 %collective-permute-done = bf16[128,1024]{1,0:T(8,128)(2,1)S(1)} collective-permute-done((bf16[128,1024]{1,0:T(8,128)(2,1)}, bf16[128,1024]{1,0:T(8,128)(2,1)S(1)}, u32[]{:S(2)}, u32[]{:S(2)}) %collective-permute-start) | collective-permute-done | bytes 262176 | tf_op jit(solution)/shard_map/ppermute | solution.py:27
  16.7 4.8 collective-permute-start.8
  26.6 4.8 collective-permute-start.9
  36.3 4.9 collective-permute-start.10
  44.7 5.0 collective-permute-start.11
  53.0 5.2 collective-permute-start.12
  62.5 5.2 collective-permute-start.13
  67.7 3.6 collective-permute-done.6
  73.1 5.2 collective-permute-start.14
  78.4 4.6 collective-permute-done.7
  96.5 5.0 gather_fusion
  101.4 7.0 %gather_fusion.4 = bf16[32,128,1024]{2,1,0:T(8,128)(2,1)} fusion(bf16[16,128,1024]{2,1,0:T(8,128)(2,1)} %gather_fusion, s32[1024]{0:T(1024)S(1)} %pad_clamp_fusion.2), kind=kCustom, calls=%fused_computation.4 | custom fusion | bytes 16777344 | tf_op jit(solution)/shard_map/gather | solution.py:96
  108.4 15.7 %all-to-all-start = ((bf16[16,1,2,128,1024]{4,3,2,1,0:T(8,128)(2,1)}), bf16[16,1,2,128,1024]{4,3,2,1,0:T(8,128)(2,1)}, u32[]{:S(2)}, u32[]{:S(2)}) async-start(bf16[16,1,2,128,1024]{4,3,2,1,0:T(8,128)(2,1)} %bitcast.133), calls=%async_computation | async-start | bytes 16777216 | tf_op jit(solution)/shard_map/all_to_all | solution.py:99
  126.0 53.5 %all-gather.2.cloned.1.call-done = bf16[2048,1024]{1,0:T(8,128)(2,1)} async-done(((bf16[128,1024]{1,0:T(8,128)(2,1)}), bf16[2048,1024]{1,0:T(8,128)(2,1)}) %all-gather.2.cloned.1.call-update) | async-done | bytes 4194320 | tf_op jit(solution)/shard_map/all_gather | solution.py:78
  179.5 7.0 %gather_fusion.8 = bf16[32,128,1024]{2,1,0:T(8,128)(2,1)} fusion(bf16[16,128,1024]{2,1,0:T(8,128)(2,1)} %bitcast.135, s32[1024]{0:T(1024)S(1)} %pad_clamp_fusion.2), kind=kCustom, calls=%fused_computation.8 | custom fusion | bytes 16777344 | tf_op jit(solution)/shard_map/gather | solution.py:95
  186.5 121.0 %all-to-all-done = bf16[16,1,2,128,1024]{4,3,2,1,0:T(8,128)(2,1)} async-done(((bf16[16,1,2,128,1024]{4,3,2,1,0:T(8,128)(2,1)}), bf16[16,1,2,128,1024]{4,3,2,1,0:T(8,128)(2,1)}, u32[]{:S(2)}, u32[]{:S(2)}) %all-to-all-start) | async-done | bytes 8388640 | tf_op jit(solution)/shard_map/all_to_all | solution.py:99
  307.5 5.6 %all-to-all-start.1 = ((bf16[16,1,2,128,1024]{4,3,2,1,0:T(8,128)(2,1)}), bf16[16,1,2,128,1024]{4,3,2,1,0:T(8,128)(2,1)}, u32[]{:S(2)}, u32[]{:S(2)}) async-start(bf16[16,1,2,128,1024]{4,3,2,1,0:T(8,128)(2,1)} %bitcast.132), calls=%async_computation.1 | async-start | bytes 16777216 | tf_op jit(solution)/shard_map/all_to_all | solution.py:98
  313.9 6.2 %gather_fusion.7 = s32[1024]{0:T(1024)S(1)} fusion(s32[32768]{0:T(1024)S(1)} %copy-done, s32[1024]{0:T(1024)S(1)} %broadcast_clamp_fusion), kind=kCustom, calls=%fused_computation.7 | custom fusion | bytes 12288 | tf_op jit(solution)/shard_map/gather | solution.py:122
  325.4 4.1 gather_fusion.6
  331.4 165.1 %all-to-all-done.1 = bf16[16,1,2,128,1024]{4,3,2,1,0:T(8,128)(2,1)} async-done(((bf16[16,1,2,128,1024]{4,3,2,1,0:T(8,128)(2,1)}), bf16[16,1,2,128,1024]{4,3,2,1,0:T(8,128)(2,1)}, u32[]{:S(2)}, u32[]{:S(2)}) %all-to-all-start.1) | async-done | bytes 8388640 | tf_op jit(solution)/shard_map/all_to_all | solution.py:98
  496.5 4.1 gather_fusion.9
  501.2 7.1 %fusion = (f32[128,8,4]{0,2,1:T(4,128)S(1)}, f32[8,1024,128,4]{2,1,3,0:T(8,128)}) fusion(pred[128,1024]{0,1:T(8,128)(4,1)S(1)} %compare_and_fusion, bf16[128,8,4,128]{3,0,2,1:T(8,128)(2,1)S(1)} %bitcast.139, bf16[1024,8,128,1]{2,1,0,3:T(8,128)(2,1)S(1)} %bitcast.136), kind=kOutput, calls=%fused_computation.12 | convolution fusion | flops 1086320640 | bytes 20070400 | tf_op jit(solution)/shard_map/rtkgd,rukd->rtkgu/dot_general | solution.py:132
  508.3 9.4 %fusion.3 = f32[128,8,4]{0,2,1:T(4,128)S(1)} fusion(f32[8,1024,128,4]{2,1,3,0:T(8,128)} %get-tuple-element.42, f32[128,8,4]{0,2,1:T(4,128)S(1)} %get-tuple-element.41, pred[128,1024]{0,1:T(8,128)(4,1)S(1)} %compare_and_fusion), kind=kLoop, calls=%fused_computation.15 | loop fusion | flops 16773120 | bytes 16941056 | tf_op jit(solution)/shard_map/reduce_sum | solution.py:138
  517.7 7.7 %fusion.9 = bf16[1,128,8,4,128]{1,4,3,2,0:T(8,128)(2,1)S(1)} fusion(f32[128,8,4]{0,2,1:T(4,128)S(1)} %fusion.3, f32[8,1024,128,4]{2,1,3,0:T(8,128)} %get-tuple-element.42, f32[128,8,4]{0,2,1:T(4,128)S(1)} %get-tuple-element.41, pred[128,1024]{0,1:T(8,128)(4,1)S(1)} %compare_and_fusion, bf16[1024,8,128,1]{2,1,0,3:T(8,128)(2,1)S(1)} %bitcast.141), kind=kOutput, calls=%fused_computation.21 | convolution fusion | flops 1091567616 | bytes 20086784 | tf_op jit(solution)/shard_map/rtkgu,rukd->rtkgd/dot_general | solution.py:139
  (107 shorter events, 48.2 us)
Async XLA Ops:
  6.5 10.1 %collective-permute-start = (bf16[128,1024]{1,0:T(8,128)(2,1)}, bf16[128,1024]{1,0:T(8,128)(2,1)S(1)}, u32[]{:S(2)}, u32[]{:S(2)}) collective-permute-start(bf16[128,1024]{1,0:T(8,128)(2,1)} %param.8), channel_id=1, source_target_pairs={{0,1},{1,2},{2,3},{3,4},{4,5},{5,6},{6,7},{7,8},{8,9},{9,10},{10,1... | collective-permute-start | bytes 786440 | tf_op jit(solution)/shard_map/ppermute | solution.py:27
  16.7 9.3 %collective-permute-start.1 = (bf16[128,1024]{1,0:T(8,128)(2,1)S(1)}, bf16[128,1024]{1,0:T(8,128)(2,1)S(1)}, u32[]{:S(2)}, u32[]{:S(2)}) collective-permute-start(bf16[128,1024]{1,0:T(8,128)(2,1)S(1)} %collective-permute-done), channel_id=1, source_target_pairs={{0,1},{1,2},{2,3},{3,4},{4,5},{5,6},{6,7},{7,8},{8,9},{9,10},{10,1... | collective-permute-start | bytes 786440 | tf_op jit(solution)/shard_map/ppermute | solution.py:27
  16.7 10.0 %collective-permute-start.8 = (bf16[128,1024]{1,0:T(8,128)(2,1)}, bf16[128,1024]{1,0:T(8,128)(2,1)S(1)}, u32[]{:S(2)}, u32[]{:S(2)}) collective-permute-start(bf16[128,1024]{1,0:T(8,128)(2,1)} %param.8), channel_id=1, source_target_pairs={{1,0},{2,1},{3,2},{4,3},{5,4},{6,5},{7,6},{8,7},{9,8},{10,9},{11,1... | collective-permute-start | bytes 786440 | tf_op jit(solution)/shard_map/ppermute | solution.py:29
  25.9 8.6 %collective-permute-start.2 = (bf16[128,1024]{1,0:T(8,128)(2,1)S(1)}, bf16[128,1024]{1,0:T(8,128)(2,1)S(1)}, u32[]{:S(2)}, u32[]{:S(2)}) collective-permute-start(bf16[128,1024]{1,0:T(8,128)(2,1)S(1)} %collective-permute-done.1), channel_id=1, source_target_pairs={{0,1},{1,2},{2,3},{3,4},{4,5},{5,6},{6,7},{7,8},{8,9},{9,10},{10,1... | collective-permute-start | bytes 786440 | tf_op jit(solution)/shard_map/ppermute | solution.py:27
  26.6 9.6 %collective-permute-start.9 = (bf16[128,1024]{1,0:T(8,128)(2,1)S(1)}, bf16[128,1024]{1,0:T(8,128)(2,1)S(1)}, u32[]{:S(2)}, u32[]{:S(2)}) collective-permute-start(bf16[128,1024]{1,0:T(8,128)(2,1)S(1)} %collective-permute-done.8), channel_id=1, source_target_pairs={{1,0},{2,1},{3,2},{4,3},{5,4},{6,5},{7,6},{8,7},{9,8},{10,9},{11,1... | collective-permute-start | bytes 786440 | tf_op jit(solution)/shard_map/ppermute | solution.py:29
  34.6 8.5 %collective-permute-start.3 = (bf16[128,1024]{1,0:T(8,128)(2,1)S(1)}, bf16[128,1024]{1,0:T(8,128)(2,1)S(1)}, u32[]{:S(2)}, u32[]{:S(2)}) collective-permute-start(bf16[128,1024]{1,0:T(8,128)(2,1)S(1)} %collective-permute-done.2), channel_id=1, source_target_pairs={{0,1},{1,2},{2,3},{3,4},{4,5},{5,6},{6,7},{7,8},{8,9},{9,10},{10,1... | collective-permute-start | bytes 786440 | tf_op jit(solution)/shard_map/ppermute | solution.py:27
  36.3 8.4 %collective-permute-start.10 = (bf16[128,1024]{1,0:T(8,128)(2,1)S(1)}, bf16[128,1024]{1,0:T(8,128)(2,1)S(1)}, u32[]{:S(2)}, u32[]{:S(2)}) collective-permute-start(bf16[128,1024]{1,0:T(8,128)(2,1)S(1)} %collective-permute-done.9), channel_id=1, source_target_pairs={{1,0},{2,1},{3,2},{4,3},{5,4},{6,5},{7,6},{8,7},{9,8},{10,9},{11,1... | collective-permute-start | bytes 786440 | tf_op jit(solution)/shard_map/ppermute | solution.py:29
  43.1 8.5 %collective-permute-start.4 = (bf16[128,1024]{1,0:T(8,128)(2,1)S(1)}, bf16[128,1024]{1,0:T(8,128)(2,1)S(1)}, u32[]{:S(2)}, u32[]{:S(2)}) collective-permute-start(bf16[128,1024]{1,0:T(8,128)(2,1)S(1)} %collective-permute-done.3), channel_id=1, source_target_pairs={{0,1},{1,2},{2,3},{3,4},{4,5},{5,6},{6,7},{7,8},{8,9},{9,10},{10,1... | collective-permute-start | bytes 786440 | tf_op jit(solution)/shard_map/ppermute | solution.py:27
  44.4 46.3 %copy-start.4 = (bf16[128,1024]{1,0:T(8,128)(2,1)S(1)}, bf16[128,1024]{1,0:T(8,128)(2,1)}, u32[]{:S(2)}) copy-start(bf16[128,1024]{1,0:T(8,128)(2,1)} %param.8) | copy-start | bytes 786436
  44.7 8.3 %collective-permute-start.11 = (bf16[128,1024]{1,0:T(8,128)(2,1)S(1)}, bf16[128,1024]{1,0:T(8,128)(2,1)S(1)}, u32[]{:S(2)}, u32[]{:S(2)}) collective-permute-start(bf16[128,1024]{1,0:T(8,128)(2,1)S(1)} %collective-permute-done.10), channel_id=1, source_target_pairs={{1,0},{2,1},{3,2},{4,3},{5,4},{6,5},{7,6},{8,7},{9,8},{10,9},{11,1... | collective-permute-start | bytes 786440 | tf_op jit(solution)/shard_map/ppermute | solution.py:29
  51.6 9.2 %collective-permute-start.5 = (bf16[128,1024]{1,0:T(8,128)(2,1)S(1)}, bf16[128,1024]{1,0:T(8,128)(2,1)S(1)}, u32[]{:S(2)}, u32[]{:S(2)}) collective-permute-start(bf16[128,1024]{1,0:T(8,128)(2,1)S(1)} %collective-permute-done.4), channel_id=1, source_target_pairs={{0,1},{1,2},{2,3},{3,4},{4,5},{5,6},{6,7},{7,8},{8,9},{9,10},{10,1... | collective-permute-start | bytes 786440 | tf_op jit(solution)/shard_map/ppermute | solution.py:27
  53.0 9.5 %collective-permute-start.12 = (bf16[128,1024]{1,0:T(8,128)(2,1)S(1)}, bf16[128,1024]{1,0:T(8,128)(2,1)S(1)}, u32[]{:S(2)}, u32[]{:S(2)}) collective-permute-start(bf16[128,1024]{1,0:T(8,128)(2,1)S(1)} %collective-permute-done.11), channel_id=1, source_target_pairs={{1,0},{2,1},{3,2},{4,3},{5,4},{6,5},{7,6},{8,7},{9,8},{10,9},{11,1... | collective-permute-start | bytes 786440 | tf_op jit(solution)/shard_map/ppermute | solution.py:29
  60.9 10.5 %collective-permute-start.6 = (bf16[128,1024]{1,0:T(8,128)(2,1)S(1)}, bf16[128,1024]{1,0:T(8,128)(2,1)}, u32[]{:S(2)}, u32[]{:S(2)}) collective-permute-start(bf16[128,1024]{1,0:T(8,128)(2,1)S(1)} %collective-permute-done.5), channel_id=1, source_target_pairs={{0,1},{1,2},{2,3},{3,4},{4,5},{5,6},{6,7},{7,8},{8,9},{9,10},{10,1... | collective-permute-start | bytes 786440 | tf_op jit(solution)/shard_map/ppermute | solution.py:27
  62.5 10.6 %collective-permute-start.13 = (bf16[128,1024]{1,0:T(8,128)(2,1)S(1)}, bf16[128,1024]{1,0:T(8,128)(2,1)S(1)}, u32[]{:S(2)}, u32[]{:S(2)}) collective-permute-start(bf16[128,1024]{1,0:T(8,128)(2,1)S(1)} %collective-permute-done.12), channel_id=1, source_target_pairs={{1,0},{2,1},{3,2},{4,3},{5,4},{6,5},{7,6},{8,7},{9,8},{10,9},{11,1... | collective-permute-start | bytes 786440 | tf_op jit(solution)/shard_map/ppermute | solution.py:29
  71.3 11.6 %collective-permute-start.7 = (bf16[128,1024]{1,0:T(8,128)(2,1)}, bf16[128,1024]{1,0:T(8,128)(2,1)}, u32[]{:S(2)}, u32[]{:S(2)}) collective-permute-start(bf16[128,1024]{1,0:T(8,128)(2,1)} %collective-permute-done.6), channel_id=1, source_target_pairs={{0,1},{1,2},{2,3},{3,4},{4,5},{5,6},{6,7},{7,8},{8,9},{9,10},{10,1... | collective-permute-start | bytes 786440 | tf_op jit(solution)/shard_map/ppermute | solution.py:27
  73.1 22.6 %collective-permute-start.14 = (bf16[128,1024]{1,0:T(8,128)(2,1)S(1)}, bf16[128,1024]{1,0:T(8,128)(2,1)S(1)}, u32[]{:S(2)}, u32[]{:S(2)}) collective-permute-start(bf16[128,1024]{1,0:T(8,128)(2,1)S(1)} %collective-permute-done.13), channel_id=1, source_target_pairs={{1,0},{2,1},{3,2},{4,3},{5,4},{6,5},{7,6},{8,7},{9,8},{10,9},{11,1... | collective-permute-start | bytes 786440 | tf_op jit(solution)/shard_map/ppermute | solution.py:29
  108.4 15.8 %copy-start.3 = (bf16[128,1024]{1,0:T(8,128)(2,1)S(1)}, bf16[128,1024]{1,0:T(8,128)(2,1)}, u32[]{:S(2)}) copy-start(bf16[128,1024]{1,0:T(8,128)(2,1)} %param.7) | copy-start | bytes 786436
  108.4 16.0 %copy-start = (s32[32768]{0:T(1024)S(1)}, s32[32768]{0:T(1024)}, u32[]{:S(2)}) copy-start(s32[32768]{0:T(1024)} %param.11) | copy-start | bytes 393220
  108.4 199.1 %all-to-all-start = ((bf16[16,1,2,128,1024]{4,3,2,1,0:T(8,128)(2,1)}), bf16[16,1,2,128,1024]{4,3,2,1,0:T(8,128)(2,1)}, u32[]{:S(2)}, u32[]{:S(2)}) async-start(bf16[16,1,2,128,1024]{4,3,2,1,0:T(8,128)(2,1)} %bitcast.133), calls=%async_computation | async-start | bytes 16777216 | tf_op jit(solution)/shard_map/all_to_all | solution.py:99
  124.1 55.4 %all-gather.2.cloned.1.call-start = ((), (), s32[]{:S(2)}) async-start(), calls=%async_computation.2 | async-start | bytes 4456448 | tf_op jit(solution)/shard_map/all_gather | solution.py:78
  307.5 189.0 %all-to-all-start.1 = ((bf16[16,1,2,128,1024]{4,3,2,1,0:T(8,128)(2,1)}), bf16[16,1,2,128,1024]{4,3,2,1,0:T(8,128)(2,1)}, u32[]{:S(2)}, u32[]{:S(2)}) async-start(bf16[16,1,2,128,1024]{4,3,2,1,0:T(8,128)(2,1)} %bitcast.132), calls=%async_computation.1 | async-start | bytes 16777216 | tf_op jit(solution)/shard_map/all_to_all | solution.py:98
  313.1 6.9 %copy-start.2 = (bf16[128,4096]{1,0:T(8,128)(2,1)S(1)}, bf16[128,4096]{1,0:T(8,128)(2,1)}, u32[]{:S(2)}) copy-start(bf16[128,4096]{1,0:T(8,128)(2,1)} %param.6) | copy-start | bytes 3145732
  320.1 0.7 copy-start.5
  508.3 9.4 %copy-start.1 = (bf16[128,8,8,128]{3,2,1,0:T(8,128)(2,1)S(1)}, bf16[128,8,8,128]{3,2,1,0:T(8,128)(2,1)}, u32[]{:S(2)}) copy-start(bf16[128,8,8,128]{3,2,1,0:T(8,128)(2,1)} %copy.49) | copy-start | bytes 6291460
Sparse Core Ops, SparseCore 0:
  127.4 52.1 all-gather.1
